TPU v7x, 128 devices: a whole 4x4x4 slice. The times are simulated.
128 devices in a mesh: slab: 16 (over y, z), col: 8 (over x, core).
Axes of the slice: x: 4, y: 4, z: 4, core: 2. Of those that a mesh axis runs over, the one named last changes fastest.
Arguments:
- dist: float32 [19, 256, 64, 1024], P(None, 'slab', None, 'col'), may hold values from 0.6 to 1.4
- fraction: bfloat16 [16, 8, 3, 3, 8, 2, 8, 128], P('slab', 'col'), may hold values from 0 to 0.5
- send_table: int32 [16, 8, 3, 3, 8], P('slab', 'col'), may hold values from -1 to 127, as said below
- recv_table: int32 [16, 8, 3, 3, 8], P('slab', 'col'), may hold values from -1 to 63, as said below
- motion: float32 [9, 256], P(None, ('slab', 'col')), as said below
Outputs:
- dist_next: float32 [19, 256, 64, 1024], P(None, 'slab', None, 'col')
- loads: float32 [6, 256], P(None, ('slab', 'col'))
Inputs may be any that keep to these rules, and one draw needn't show every extreme that they name: `send_table`: entry (p, q, a, b, j) is -1 for an empty slot, else s * 64 + k: owned sphere s of device (p, q) covers block k of the device at offset (a - 1, b - 1) along slab and col, taken periodically. Blocks of a device are numbered x-block * 8 + z-block. `recv_table`: entry (p, q, a, b, j) equals send_table[p + a - 1, q + b - 1, 2 - a, 2 - b, j] mod 64 where that entry is live and -1 where it is empty, indices taken periodically. No block of a device is covered by more than two live slots. Some device has all of its 72 incoming slots live. `motion`: rows 0 to 2: sphere centre in cells from the owner's first cell, within [0, 16), [0, 128), [0, 64); rows 3 to 5 velocity; rows 6 to 8 angular velocity.
All inputs are finite; a program needn't handle non-finite values.
Results may differ from a plain program's by a relative error of at most 0.00055.
Values may be sent and summed in bfloat16 or wider, within the bound.
A program may use at most 256 MiB of HBM per device.

v0:
```python
import functools

import jax
import jax.numpy as jnp
from jax import lax
from jax.experimental import pallas as pl
from jax.experimental.pallas import tpu as pltpu
from jax.sharding import PartitionSpec as P

F32 = jnp.float32
MESH = pl.DeviceIdType.MESH
TAU = 0.9
GAP = TAU - 0.5

AXIS_PAIRS = [(1, 2, 0), (3, 4, 1), (5, 6, 2)]
PLANE_PAIRS = [(7, 8, 9, 10, 0, 1), (11, 12, 13, 14, 0, 2), (15, 16, 17, 18, 1, 2)]
VEL = [
    (0, 0, 0),
    (1, 0, 0), (-1, 0, 0), (0, 1, 0), (0, -1, 0), (0, 0, 1), (0, 0, -1),
    (1, 1, 0), (-1, -1, 0), (1, -1, 0), (-1, 1, 0),
    (1, 0, 1), (-1, 0, -1), (1, 0, -1), (-1, 0, 1),
    (0, 1, 1), (0, -1, -1), (0, 1, -1), (0, -1, 1),
]
OPP = [0, 2, 1, 4, 3, 6, 5, 8, 7, 10, 9, 12, 11, 14, 13, 16, 15, 18, 17]
KEPT = [1, 7, 9, 11, 13, 2, 8, 10, 12, 14, 0, 3, 4, 5, 6, 15, 16, 17, 18]
SLOT = {pop: place for place, pop in enumerate(KEPT)}
RISING = [3, 7, 10, 15, 17]
FALLING = [4, 8, 9, 16, 18]
CORNERS = [(7, 1, 1), (10, -1, 1), (9, 1, -1), (8, -1, -1)]
OFFSETS = [(a, b) for a in range(3) for b in range(3) if (a, b) != (1, 1)]
N_FIELD = 7


def step_kernel(
    sizes, dist_hbm, frac_hbm, send_ref, recv_ref, motion_ref,
    post_ref, yin_ref, total_ref,
    cells_buf, fluid_buf, frac_in, par_out, par_in, slot_buf, table_v, table_s,
    ypack, corner_out, corner_in, part_out, part_in,
    dist_sem, frac_send, frac_recv, par_send, par_recv, local_sem,
    xr_send, xr_recv, yr_send, yr_recv, cr_send, cr_recv, ld_send, ld_recv,
):
    slabs, cols, nx, nz, ny, kd = sizes
    nbx, nbz = nx // 2, nz // 8
    slots = 9 * kd
    me_p, me_q = lax.axis_index("slab"), lax.axis_index("col")

    def at(dp, dq):
        return (lax.rem(me_p + (dp + slabs), slabs), lax.rem(me_q + (dq + cols), cols))

    def remote(src, dst, send_sem, recv_sem, dp, dq):
        return pltpu.make_async_remote_copy(
            src_ref=src, dst_ref=dst, send_sem=send_sem, recv_sem=recv_sem,
            device_id=at(dp, dq), device_id_type=MESH,
        )

    def row_of(step):
        return lax.rem(nbx - step, nbx)

    def dist_copy(step):
        rows = pl.ds(row_of(step) * 2, 2)
        return pltpu.make_async_copy(
            dist_hbm.at[:, rows], cells_buf.at[:, rows], dist_sem.at[step]
        )

    barrier = pltpu.get_barrier_semaphore()
    for a, b in OFFSETS:
        pl.semaphore_signal(barrier, inc=1, device_id=at(a - 1, b - 1), device_id_type=MESH)

    for step in range(nbx):
        dist_copy(step).start()
    own_copy = pltpu.make_async_copy(frac_hbm.at[0, 0, 1, 1], frac_in.at[4], local_sem.at[0])
    own_copy.start()

    lane = lax.broadcasted_iota(jnp.int32, (8, 128), 1)
    sub = lax.broadcasted_iota(jnp.int32, (8, 128), 0)

    base = jnp.zeros((8, 128), F32)
    for s in range(2):
        for r in range(9):
            base = jnp.where(lane == 9 * s + r, motion_ref[s, r], base)
    for a in range(3):
        for b in range(3):
            row = base
            for j in range(kd):
                second = (send_ref[0, a, b, 0, j] >= nbx * nbz).astype(F32)
                row = jnp.where(lane == 18 + j, second, row)
            if (a, b) == (1, 1):
                par_in[4] = row
            else:
                par_out[a * 3 + b] = row

    pl.semaphore_wait(barrier, len(OFFSETS))
    payload = {}
    for a, b in OFFSETS:
        out, land = a * 3 + b, (2 - a) * 3 + (2 - b)
        payload[land] = (
            remote(frac_hbm.at[0, 0, a, b], frac_in.at[land],
                   frac_send.at[out], frac_recv.at[land], a - 1, b - 1),
            remote(par_out.at[out], par_in.at[land],
                   par_send.at[out], par_recv.at[land], a - 1, b - 1),
        )
        for copy in payload[land]:
            copy.start()

    first = jnp.full((8, 128), slots, jnp.int32)
    other = jnp.full((8, 128), slots, jnp.int32)
    for n in range(9):
        for j in range(kd):
            hit = lane == recv_ref[0, n // 3, n % 3, 0, j]
            free = first == slots
            other = jnp.where(hit & jnp.logical_not(free), n * kd + j, other)
            first = jnp.where(hit & free, n * kd + j, first)
    table_v[0] = first
    table_v[1] = other
    table_copy = pltpu.make_async_copy(table_v, table_s, local_sem.at[1])
    table_copy.start()
    for c in range(N_FIELD):
        slot_buf[slots, c] = jnp.zeros((8, 128), F32)
    ypack[...] = jnp.zeros_like(ypack)

    def moments_row(step, _):
        dist_copy(step).wait()
        bx = row_of(step)

        def moments_block(bz, _):
            rows = pl.ds(pl.multiple_of(bz * 8, 8), 8)
            for dx in range(2):
                x = bx * 2 + dx
                plus, minus = {}, {}
                for i in range(1, 19, 2):
                    ahead = cells_buf[i, x, rows, :]
                    back = cells_buf[i + 1, x, rows, :]
                    plus[i] = ahead + back
                    minus[i] = ahead - back
                    cells_buf[i, x, rows, :] = plus[i]
                    cells_buf[i + 1, x, rows, :] = minus[i]
                density = cells_buf[0, x, rows, :]
                for i in range(1, 19, 2):
                    density = density + plus[i]
                inverse = 1.0 / density
                mom_x = (minus[1] + (minus[7] + minus[9])) + (minus[11] + minus[13])
                mom_y = (minus[3] + (minus[7] - minus[9])) + (minus[15] + minus[17])
                mom_z = (minus[5] + (minus[11] - minus[13])) + (minus[15] - minus[17])
                block = bx * nbz + bz
                fluid_buf[block, 0, dx] = density
                fluid_buf[block, 1, dx] = mom_x * inverse
                fluid_buf[block, 2, dx] = mom_y * inverse
                fluid_buf[block, 3, dx] = mom_z * inverse
            return 0

        return lax.fori_loop(0, nbz, moments_block, 0)

    lax.fori_loop(0, nbx, moments_row, 0)

    own_copy.wait()
    for pair in payload.values():
        for copy in pair:
            copy.wait_recv()

    pos_y = lane.astype(F32) + 0.5
    pos_z = sub.astype(F32) + 0.5

    def slot_place(n, j):
        block = recv_ref[0, n // 3, n % 3, 0, j]
        return block >= 0, jnp.maximum(block, 0)

    def spread(row, place):
        return jnp.broadcast_to(row[:, place:place + 1], (8, 128))

    def slot_sphere(row, j, both):
        second = spread(row, 18 + j) > 0.5
        return second, [jnp.where(second, both[9 + r], both[r]) for r in range(len(both) - 9)]

    def levers(n, safe, centre):
        a, b = n // 3, n % 3
        from_x = ((1 - a) * nx + lax.div(safe, nbz) * 2).astype(F32)
        from_y = ((1 - b) * ny).astype(F32)
        from_z = (lax.rem(safe, nbz) * 8).astype(F32)
        scale = 1.0 / ny
        lever_x = [((from_x + (dx + 0.5)) - centre[0]) * scale for dx in range(2)]
        lever_y = ((pos_y + from_y) - centre[1]) * scale
        lever_z = ((pos_z + from_z) - centre[2]) * scale
        return lever_x, lever_y, lever_z

    def rounded(value):
        return value.astype(jnp.bfloat16).astype(F32)

    def slots_of(n, _):
        row = par_in[n]
        both = [spread(row, r) for r in range(18)]
        for j in range(kd):
            live, safe = slot_place(n, j)
            _, prm = slot_sphere(row, j, both)
            lever_x, lever_y, lever_z = levers(n, safe, prm)
            vx, vy, vz, wx, wy, wz = prm[3:9]
            slot = n * kd + j
            slot_buf[slot, 2] = rounded(vx + (wy * lever_z - wz * lever_y))
            for dx in range(2):
                frac = frac_in[n, j, dx].astype(F32)
                weight = frac * GAP / ((1.0 - frac) + GAP)
                slot_buf[slot, dx] = jnp.where(live, weight, 0.0)
                slot_buf[slot, 3 + dx] = rounded(vy + (wz * lever_x[dx] - wx * lever_z))
                slot_buf[slot, 5 + dx] = rounded(vz + (wx * lever_y - wy * lever_x[dx]))
        return 0

    lax.fori_loop(0, 9, slots_of, 0)
    table_copy.wait()

    def collide_block(bx, bz):
        rows = pl.ds(pl.multiple_of(bz * 8, 8), 8)
        block = bx * nbz + bz
        one, two = table_s[0, 0, block], table_s[1, 0, block]
        up, down = jnp.zeros((8, 128), F32), jnp.zeros((8, 128), F32)
        for dx in range(2):
            x = bx * 2 + dx
            fields = []
            for slot in (one, two):
                weight = slot_buf[slot, dx]
                flow = [slot_buf[slot, 2], slot_buf[slot, 3 + dx], slot_buf[slot, 5 + dx]]
                first_m = [weight * f for f in flow]
                second_m = [
                    first_m[0] * flow[0], first_m[1] * flow[1], first_m[2] * flow[2],
                    first_m[0] * flow[1], first_m[0] * flow[2], first_m[1] * flow[2],
                ]
                fields.append([weight] + first_m + second_m)
            total = [u + v for u, v in zip(*fields)]
            solid = total[0]
            density = fluid_buf[block, 0, dx]
            vel = [fluid_buf[block, 1 + c, dx] for c in range(3)]
            relax = (1.0 - solid) * (1.0 / TAU)
            keep = 0.5 - 0.5 * relax
            keep_odd = keep - solid
            even_rho = (relax - solid) * density
            odd_rho = (relax + solid) * density
            scaled = [even_rho * v for v in vel]
            flux = [odd_rho * vel[c] + density * total[1 + c] for c in range(3)]
            t_xx = scaled[0] * vel[0] + density * total[4]
            t_yy = scaled[1] * vel[1] + density * total[5]
            t_zz = scaled[2] * vel[2] + density * total[6]
            t_xy = scaled[0] * vel[1] + density * total[7]
            t_xz = scaled[0] * vel[2] + density * total[8]
            t_yz = scaled[1] * vel[2] + density * total[9]
            rest = relax * density - 1.5 * ((t_xx + t_yy) + t_zz)
            outs = {0: (keep + keep) * cells_buf[0, x, rows, :] + (1.0 / 3.0) * rest}
            rest_axis = (1.0 / 18.0) * rest
            rest_plane = (1.0 / 36.0) * rest
            diag = [t_xx, t_yy, t_zz]
            for i, back, c in AXIS_PAIRS:
                even = keep * cells_buf[i, x, rows, :] + (rest_axis + 0.25 * diag[c])
                odd = keep_odd * cells_buf[i + 1, x, rows, :] + (1.0 / 6.0) * flux[c]
                outs[i] = even + odd
                outs[back] = even - odd
            eighth = [0.125 * d for d in diag]
            twelfth = [(1.0 / 12.0) * f for f in flux]
            cross = {(0, 1): t_xy, (0, 2): t_xz, (1, 2): t_yz}
            for i, i_back, j, j_back, c, d in PLANE_PAIRS:
                middle = rest_plane + (eighth[c] + eighth[d])
                tilt = 0.25 * cross[(c, d)]
                even = keep * cells_buf[i, x, rows, :] + (middle + tilt)
                odd = keep_odd * cells_buf[i + 1, x, rows, :] + (twelfth[c] + twelfth[d])
                outs[i] = even + odd
                outs[i_back] = even - odd
                even = keep * cells_buf[j, x, rows, :] + (middle - tilt)
                odd = keep_odd * cells_buf[j + 1, x, rows, :] + (twelfth[c] - twelfth[d])
                outs[j] = even + odd
                outs[j_back] = even - odd
            for m in range(5):
                place = dx * 5 + m
                rise, fall = outs[RISING[m]], outs[FALLING[m]]
                up = jnp.where(lane == place, pltpu.roll(rise, 1 + place, 1), up)
                down = jnp.where(
                    lane == place, fall if place == 0 else pltpu.roll(fall, place, 1), down
                )
                outs[RISING[m]] = pltpu.roll(rise, 1, 1)
                outs[FALLING[m]] = pltpu.roll(fall, 127, 1)
            for pop in range(19):
                post_ref[SLOT[pop], x + 1, rows, :] = outs[pop]
        start = (2 * bx + 1) * 5
        mine = (lane >= start) & (lane < start + 10)
        ypack[0, rows, :] = jnp.where(mine, pltpu.roll(up, start, 1), ypack[0, rows, :])
        ypack[1, rows, :] = jnp.where(mine, pltpu.roll(down, start, 1), ypack[1, rows, :])

    def collide_row(step, _):
        bx = row_of(step)

        def body(bz, _):
            collide_block(bx, bz)
            return 0

        return lax.fori_loop(0, nbz, body, 0)

    lax.fori_loop(0, 2, collide_row, 0)

    x_copies = [
        remote(post_ref.at[pl.ds(0, 5), nx], post_ref.at[pl.ds(0, 5), 0],
               xr_send.at[0], xr_recv.at[0], 1, 0),
        remote(post_ref.at[pl.ds(5, 5), 1], post_ref.at[pl.ds(5, 5), nx + 1],
               xr_send.at[1], xr_recv.at[1], -1, 0),
    ]
    for copy in x_copies:
        copy.start()
    corner_copies = []
    for n, (pop, sx, sy) in enumerate(CORNERS):
        line = jnp.zeros((8, 128), F32)
        edge = 0 if sy == 1 else 127
        for bz in range(nbz):
            part = post_ref[SLOT[pop], nx if sx == 1 else 1, pl.ds(bz * 8, 8), :]
            shift = (bz - edge) % 128
            line = jnp.where(lane == bz, part if shift == 0 else pltpu.roll(part, shift, 1), line)
        corner_out[n] = line
        copy = remote(corner_out.at[n], corner_in.at[n], cr_send.at[n], cr_recv.at[n], sx, sy)
        copy.start()
        corner_copies.append(copy)

    lax.fori_loop(2, nbx, collide_row, 0)

    y_copies = [
        remote(ypack.at[0], yin_ref.at[0], yr_send.at[0], yr_recv.at[0], 0, 1),
        remote(ypack.at[1], yin_ref.at[1], yr_send.at[1], yr_recv.at[1], 0, -1),
    ]
    for copy in y_copies:
        copy.start()

    def loads_of(n, _):
        row = par_in[n]
        both = [spread(row, 9 * s + r) for s in range(2) for r in range(3)]
        acc = [jnp.zeros((8, 128), F32) for _ in range(12)]
        for j in range(kd):
            _, safe = slot_place(n, j)
            second = spread(row, 18 + j) > 0.5
            centre = [jnp.where(second, both[3 + r], both[r]) for r in range(3)]
            lever_x, lever_y, lever_z = levers(n, safe, centre)
            slot = n * kd + j
            push, turn_y, turn_z = [], 0.0, 0.0
            for dx in range(2):
                wr = slot_buf[slot, dx] * fluid_buf[safe, 0, dx]
                px = wr * (slot_buf[slot, 2] - fluid_buf[safe, 1, dx])
                py = wr * (slot_buf[slot, 3 + dx] - fluid_buf[safe, 2, dx])
                pz = wr * (slot_buf[slot, 5 + dx] - fluid_buf[safe, 3, dx])
                push.append((px, py, pz))
                turn_y = turn_y - lever_x[dx] * pz
                turn_z = turn_z + lever_x[dx] * py
            px, py, pz = [u + v for u, v in zip(*push)]
            values = [
                px, py, pz,
                lever_y * pz - lever_z * py,
                turn_y + lever_z * px,
                turn_z - lever_y * px,
            ]
            for c, value in enumerate(values):
                acc[c] = acc[c] + jnp.where(second, 0.0, value)
                acc[6 + c] = acc[6 + c] + jnp.where(second, value, 0.0)
        for s in range(2):
            stack = jnp.zeros((8, 128), F32)
            for c in range(6):
                total = jnp.sum(acc[6 * s + c], axis=0, keepdims=True)
                stack = jnp.where(sub == c, total, stack)
            part_out[n, pl.ds(8 * s, 8), :] = stack
        return 0

    lax.fori_loop(0, 9, loads_of, 0)
    load_copies = []
    for a, b in OFFSETS:
        out, land = a * 3 + b, (2 - a) * 3 + (2 - b)
        copy = remote(part_out.at[out], part_in.at[land],
                      ld_send.at[out], ld_recv.at[land], a - 1, b - 1)
        copy.start()
        load_copies.append((land, copy))
    total = part_out[4]
    for land, copy in load_copies:
        copy.wait_recv()
        total = total + part_in[land]
    total_ref[...] = total

    for copy in corner_copies + y_copies + x_copies:
        copy.wait_recv()
    for n, (pop, sx, sy) in enumerate(CORNERS):
        way = 0 if sy == 1 else 1
        place = (RISING if sy == 1 else FALLING).index(pop) + (0 if sx == 1 else (nx + 1) * 5)
        line = corner_in[n]
        for bz in range(nbz):
            rows = pl.ds(bz * 8, 8)
            moved = pltpu.roll(line, (place - bz) % 128, 1)
            yin_ref[way, rows, :] = jnp.where(lane == place, moved, yin_ref[way, rows, :])

    for pair in payload.values():
        for copy in pair:
            copy.wait_send()
    for copy in x_copies + corner_copies + y_copies:
        copy.wait_send()
    for _, copy in load_copies:
        copy.wait_send()


def stream_kernel(nz, ny, post_ref, yin_ref, total_ref, out_ref, loads_ref):
    step = pl.program_id(0)
    @pl.when(step == 0)
    def _():
        total = jnp.sum(total_ref[...], axis=1, keepdims=True) * (-1.0 / (2 * 8 * ny))
        place_s = lax.broadcasted_iota(jnp.int32, (2, 6), 0)
        place_c = lax.broadcasted_iota(jnp.int32, (2, 6), 1)
        result = jnp.zeros((2, 6), F32)
        for s in range(2):
            for c in range(6):
                value = jnp.broadcast_to(total[8 * s + c:8 * s + c + 1], (2, 6))
                result = jnp.where((place_s == s) & (place_c == c), value, result)
        loads_ref[...] = result

    lane = lax.broadcasted_iota(jnp.int32, (nz, ny), 1)
    row = lax.broadcasted_iota(jnp.int32, (nz, ny), 0)
    up, down = yin_ref[0], yin_ref[1]
    for dx in range(2):
        x = step * 2 + dx
        for pop in range(19):
            cx, cy, cz = VEL[pop]
            plane = post_ref[SLOT[pop], x + 1 - cx]
            if cy == 1:
                place = (x + 1 - cx) * 5 + RISING.index(pop)
                plane = jnp.where(lane == 0, pltpu.roll(up, 128 - place, 1), plane)
            elif cy == -1:
                place = (x + 1 - cx) * 5 + FALLING.index(pop)
                plane = jnp.where(lane == 127, pltpu.roll(down, 127 - place, 1), plane)
            if cz != 0:
                back = post_ref[SLOT[OPP[pop]], x + 1]
                if cy != 0:
                    back = pltpu.roll(back, 1 if cy == 1 else 127, 1)
                plane = jnp.where(
                    row == (0 if cz == 1 else nz - 1), back,
                    pltpu.roll(plane, 1 if cz == 1 else nz - 1, 0),
                )
            out_ref[pop, dx] = plane


def per_device(mesh_sizes, dist, fraction, send_table, recv_table, motion):
    slabs, cols = mesh_sizes
    nx, nz, ny = dist.shape[1:]
    kd = fraction.shape[4]
    slots = 9 * kd
    blocks = (nx // 2) * (nz // 8)
    hbm = pl.BlockSpec(memory_space=pltpu.HBM)
    smem = pl.BlockSpec(memory_space=pltpu.SMEM)
    vmem = pl.BlockSpec(memory_space=pltpu.VMEM)
    dma = pltpu.SemaphoreType.DMA
    post, yin, total = pl.pallas_call(
        functools.partial(step_kernel, (slabs, cols, nx, nz, ny, kd)),
        out_shape=[
            pltpu.VMEM((19, nx + 2, nz, ny), F32),
            pltpu.VMEM((2, nz, ny), F32),
            pltpu.VMEM((16, 128), F32),
        ],
        in_specs=[hbm, hbm, smem, smem, smem],
        out_specs=[vmem, vmem, vmem],
        scratch_shapes=[
            pltpu.VMEM((19, nx, nz, ny), F32),
            pltpu.VMEM((blocks, 4, 2, 8, ny), F32),
            pltpu.VMEM((9, kd, 2, 8, ny), jnp.bfloat16),
            pltpu.VMEM((9, 8, 128), F32),
            pltpu.VMEM((9, 8, 128), F32),
            pltpu.VMEM((slots + 1, N_FIELD, 8, ny), F32),
            pltpu.VMEM((2, 8, 128), jnp.int32),
            pltpu.SMEM((2, 8, 128), jnp.int32),
            pltpu.VMEM((2, nz, ny), F32),
            pltpu.VMEM((4, 8, 128), F32),
            pltpu.VMEM((4, 8, 128), F32),
            pltpu.VMEM((9, 16, 128), F32),
            pltpu.VMEM((9, 16, 128), F32),
            dma((nx // 2,)), dma((9,)), dma((9,)), dma((9,)), dma((9,)), dma((2,)),
            dma((2,)), dma((2,)), dma((2,)), dma((2,)), dma((4,)), dma((4,)),
            dma((9,)), dma((9,)),
        ],
        compiler_params=pltpu.CompilerParams(
            collective_id=0, has_side_effects=True, vmem_limit_bytes=44 << 20
        ),
        name="collide_exchange",
    )(dist, fraction, *(jnp.transpose(t, (0, 2, 3, 1, 4)) for t in (send_table, recv_table)), motion.T)
    dist_next, loads = pl.pallas_call(
        functools.partial(stream_kernel, nz, ny),
        grid=(nx // 2,),
        out_shape=[jax.ShapeDtypeStruct(dist.shape, F32), jax.ShapeDtypeStruct((2, 6), F32)],
        in_specs=[vmem, vmem, vmem],
        out_specs=[
            pl.BlockSpec((19, 2, nz, ny), lambda step: (0, step, 0, 0)),
            pl.BlockSpec((2, 6), lambda step: (0, 0)),
        ],
        compiler_params=pltpu.CompilerParams(vmem_limit_bytes=8 << 20),
        name="stream",
    )(post, yin, total)
    return (dist_next, loads.T)


def solution(mesh):
    placed = (
        P(None, "slab", None, "col"),
        P("slab", "col", None, None, None, None, None, None),
        P("slab", "col", None, None, None),
        P("slab", "col", None, None, None),
        P(None, ("slab", "col")),
    )
    return jax.shard_map(
        functools.partial(per_device, (mesh.shape["slab"], mesh.shape["col"])),
        mesh=mesh,
        in_specs=placed,
        out_specs=(P(None, "slab", None, "col"), P(None, ("slab", "col"))),
        check_vma=False,
    )
```

profile of v0, /device:TPU:1, one launch (start us, length us, event | category | flops | bytes accessed | tf_op | source)
XLA Modules:
  0.0 42.5 jit_solution(12547608799128187925)
XLA Ops:
  0.6 36.2 %collide_exchange.1 = (f32[19,18,64,128]{3,2,1,0:T(8,128)S(1)}, f32[2,64,128]{2,1,0:T(8,128)S(1)}, f32[16,128]{1,0:T(8,128)S(1)}) custom-call(f32[19,16,64,128]{3,2,1,0:T(8,128)} %dist_hbm.1, bf16[1,1,3,3,8,2,8,128]{7,6,5,4,3,2,1,0:T(8,128)(2,1)} %frac_hbm.1, s32[1,3,3,1,8]{4,3,2,1,0:T(1,128)} %bitcast.4, s32[1,3,3,1,8]{4,3,2,1,0:T(1,128)} %bitcast.5, ...), custom_call_target="tpu_custom_call" | custom-call | tf_op jit(solution)/shard_map/collide_exchange/pallas_call | solution.py:444
  36.8 5.7 %stream.1 = (f32[19,16,64,128]{3,2,1,0:T(8,128)}, f32[2,6]{1,0:T(2,128)}) custom-call(f32[19,18,64,128]{3,2,1,0:T(8,128)S(1)} %get-tuple-element.7.post_ref, f32[2,64,128]{2,1,0:T(8,128)S(1)} %get-tuple-element.8.yin_ref, f32[16,128]{1,0:T(8,128)S(1)} %get-tuple-element.9.total_ref), custom_call_target="tpu_custom_call" | custom-call | tf_op jit(solution)/shard_map/stream/pallas_call | solution.py:476
where the time goes:
time: 42.6 us; the launch traced here: 42.5 us
  Pallas kernels  41.8 us (98%)
  between operations  0.64 us (2%)
    pallas_call x1, Pallas kernels, per_device(): pl.pallas_call(functools.partial(step_kernel, (slabs, cols, nx, nz, ny, k...  36.2 us
    pallas_call x1, Pallas kernels, per_device(): pl.pallas_call(functools.partial(stream_kernel, nz, ny), grid=(nx // 2,),...  5.66 us

commit v1 on v0

--- a/solution.py
+++ b/solution.py
@@ -152,11 +152,6 @@
 
     lax.fori_loop(0, nbx, moments_row, 0)
 
-    own_copy.wait()
-    for pair in payload.values():
-        for copy in pair:
-            copy.wait_recv()
-
     pos_y = lane.astype(F32) + 0.5
     pos_z = sub.astype(F32) + 0.5
 
@@ -185,7 +180,20 @@
     def rounded(value):
         return value.astype(jnp.bfloat16).astype(F32)
 
-    def slots_of(n, _):
+    def slots_of(step, _):
+        n = lax.rem(step + 3, 9)
+
+        @pl.when(step == 0)
+        def _():
+            own_copy.wait()
+
+        for group in range(3):
+            @pl.when(step == 3 * group)
+            def _():
+                for land in range(3 * ((group + 1) % 3), 3 * ((group + 1) % 3) + 3):
+                    for copy in payload.get(land, ()):
+                        copy.wait_recv()
+
         row = par_in[n]
         both = [spread(row, r) for r in range(18)]
         for j in range(kd):
@@ -210,7 +218,6 @@
         rows = pl.ds(pl.multiple_of(bz * 8, 8), 8)
         block = bx * nbz + bz
         one, two = table_s[0, 0, block], table_s[1, 0, block]
-        up, down = jnp.zeros((8, 128), F32), jnp.zeros((8, 128), F32)
         for dx in range(2):
             x = bx * 2 + dx
             fields = []
@@ -264,21 +271,25 @@
                 odd = keep_odd * cells_buf[j + 1, x, rows, :] + (twelfth[c] - twelfth[d])
                 outs[j] = even + odd
                 outs[j_back] = even - odd
-            for m in range(5):
-                place = dx * 5 + m
-                rise, fall = outs[RISING[m]], outs[FALLING[m]]
-                up = jnp.where(lane == place, pltpu.roll(rise, 1 + place, 1), up)
-                down = jnp.where(
-                    lane == place, fall if place == 0 else pltpu.roll(fall, place, 1), down
-                )
-                outs[RISING[m]] = pltpu.roll(rise, 1, 1)
-                outs[FALLING[m]] = pltpu.roll(fall, 127, 1)
             for pop in range(19):
                 post_ref[SLOT[pop], x + 1, rows, :] = outs[pop]
+
+    lane_z = lax.broadcasted_iota(jnp.int32, (nz, 128), 1)
+
+    def pack_row(bx):
         start = (2 * bx + 1) * 5
-        mine = (lane >= start) & (lane < start + 10)
-        ypack[0, rows, :] = jnp.where(mine, pltpu.roll(up, start, 1), ypack[0, rows, :])
-        ypack[1, rows, :] = jnp.where(mine, pltpu.roll(down, start, 1), ypack[1, rows, :])
+        mine = (lane_z >= start) & (lane_z < start + 10)
+        for way, (pops, edge) in enumerate(((RISING, 127), (FALLING, 0))):
+            packed = jnp.zeros((nz, 128), F32)
+            for dx in range(2):
+                for m in range(5):
+                    plane = post_ref[SLOT[pops[m]], bx * 2 + dx + 1]
+                    place = dx * 5 + m
+                    shift = (place - edge) % 128
+                    packed = jnp.where(
+                        lane_z == place, plane if shift == 0 else pltpu.roll(plane, shift, 1), packed
+                    )
+            ypack[way] = jnp.where(mine, pltpu.roll(packed, start, 1), ypack[way])
 
     def collide_row(step, _):
         bx = row_of(step)
@@ -287,9 +298,18 @@
             collide_block(bx, bz)
             return 0
 
-        return lax.fori_loop(0, nbz, body, 0)
-
-    lax.fori_loop(0, 2, collide_row, 0)
+        lax.fori_loop(0, nbz, body, 0)
+
+        @pl.when(step == 0)
+        def _():
+            x_copies[1].start()
+
+        @pl.when(step == 1)
+        def _():
+            x_copies[0].start()
+
+        pack_row(bx)
+        return 0
 
     x_copies = [
         remote(post_ref.at[pl.ds(0, 5), nx], post_ref.at[pl.ds(0, 5), 0],
@@ -297,12 +317,12 @@
         remote(post_ref.at[pl.ds(5, 5), 1], post_ref.at[pl.ds(5, 5), nx + 1],
                xr_send.at[1], xr_recv.at[1], -1, 0),
     ]
-    for copy in x_copies:
-        copy.start()
+    lax.fori_loop(0, 2, collide_row, 0)
+
     corner_copies = []
     for n, (pop, sx, sy) in enumerate(CORNERS):
         line = jnp.zeros((8, 128), F32)
-        edge = 0 if sy == 1 else 127
+        edge = 127 if sy == 1 else 0
         for bz in range(nbz):
             part = post_ref[SLOT[pop], nx if sx == 1 else 1, pl.ds(bz * 8, 8), :]
             shift = (bz - edge) % 128
@@ -311,15 +331,6 @@
         copy = remote(corner_out.at[n], corner_in.at[n], cr_send.at[n], cr_recv.at[n], sx, sy)
         copy.start()
         corner_copies.append(copy)
-
-    lax.fori_loop(2, nbx, collide_row, 0)
-
-    y_copies = [
-        remote(ypack.at[0], yin_ref.at[0], yr_send.at[0], yr_recv.at[0], 0, 1),
-        remote(ypack.at[1], yin_ref.at[1], yr_send.at[1], yr_recv.at[1], 0, -1),
-    ]
-    for copy in y_copies:
-        copy.start()
 
     def loads_of(n, _):
         row = par_in[n]
@@ -366,6 +377,16 @@
                       ld_send.at[out], ld_recv.at[land], a - 1, b - 1)
         copy.start()
         load_copies.append((land, copy))
+
+    lax.fori_loop(2, nbx, collide_row, 0)
+
+    y_copies = [
+        remote(ypack.at[0], yin_ref.at[0], yr_send.at[0], yr_recv.at[0], 0, 1),
+        remote(ypack.at[1], yin_ref.at[1], yr_send.at[1], yr_recv.at[1], 0, -1),
+    ]
+    for copy in y_copies:
+        copy.start()
+
     total = part_out[4]
     for land, copy in load_copies:
         copy.wait_recv()
@@ -392,43 +413,56 @@
         copy.wait_send()
 
 
-def stream_kernel(nz, ny, post_ref, yin_ref, total_ref, out_ref, loads_ref):
-    step = pl.program_id(0)
-    @pl.when(step == 0)
-    def _():
-        total = jnp.sum(total_ref[...], axis=1, keepdims=True) * (-1.0 / (2 * 8 * ny))
-        place_s = lax.broadcasted_iota(jnp.int32, (2, 6), 0)
-        place_c = lax.broadcasted_iota(jnp.int32, (2, 6), 1)
-        result = jnp.zeros((2, 6), F32)
-        for s in range(2):
-            for c in range(6):
-                value = jnp.broadcast_to(total[8 * s + c:8 * s + c + 1], (2, 6))
-                result = jnp.where((place_s == s) & (place_c == c), value, result)
-        loads_ref[...] = result
-
+def stream_kernel(
+    nx, nz, ny, post_ref, yin_ref, total_ref, out_hbm, loads_ref, planes, out_sem
+):
     lane = lax.broadcasted_iota(jnp.int32, (nz, ny), 1)
     row = lax.broadcasted_iota(jnp.int32, (nz, ny), 0)
-    up, down = yin_ref[0], yin_ref[1]
-    for dx in range(2):
-        x = step * 2 + dx
+
+    def copy_out(x):
+        return pltpu.make_async_copy(planes.at[:, x], out_hbm.at[:, x], out_sem.at[x])
+
+    def plane_of(x, _):
+        up, down = yin_ref[0], yin_ref[1]
         for pop in range(19):
             cx, cy, cz = VEL[pop]
             plane = post_ref[SLOT[pop], x + 1 - cx]
             if cy == 1:
                 place = (x + 1 - cx) * 5 + RISING.index(pop)
-                plane = jnp.where(lane == 0, pltpu.roll(up, 128 - place, 1), plane)
+                plane = jnp.where(
+                    lane == 0, pltpu.roll(up, 128 - place, 1), pltpu.roll(plane, 1, 1)
+                )
             elif cy == -1:
                 place = (x + 1 - cx) * 5 + FALLING.index(pop)
-                plane = jnp.where(lane == 127, pltpu.roll(down, 127 - place, 1), plane)
+                plane = jnp.where(
+                    lane == 127, pltpu.roll(down, 127 - place, 1), pltpu.roll(plane, 127, 1)
+                )
             if cz != 0:
                 back = post_ref[SLOT[OPP[pop]], x + 1]
-                if cy != 0:
-                    back = pltpu.roll(back, 1 if cy == 1 else 127, 1)
                 plane = jnp.where(
                     row == (0 if cz == 1 else nz - 1), back,
                     pltpu.roll(plane, 1 if cz == 1 else nz - 1, 0),
                 )
-            out_ref[pop, dx] = plane
+            planes[pop, x] = plane
+        copy_out(x).start()
+        return 0
+
+    lax.fori_loop(0, nx, plane_of, 0)
+    total = jnp.sum(total_ref[...], axis=1, keepdims=True) * (-1.0 / (2 * 8 * ny))
+    place_s = lax.broadcasted_iota(jnp.int32, (2, 6), 0)
+    place_c = lax.broadcasted_iota(jnp.int32, (2, 6), 1)
+    result = jnp.zeros((2, 6), F32)
+    for s in range(2):
+        for c in range(6):
+            value = jnp.broadcast_to(total[8 * s + c:8 * s + c + 1], (2, 6))
+            result = jnp.where((place_s == s) & (place_c == c), value, result)
+    loads_ref[...] = result
+
+    def finish(x, _):
+        copy_out(x).wait()
+        return 0
+
+    lax.fori_loop(0, nx, finish, 0)
 
 
 def per_device(mesh_sizes, dist, fraction, send_table, recv_table, motion):
@@ -474,15 +508,12 @@
         name="collide_exchange",
     )(dist, fraction, *(jnp.transpose(t, (0, 2, 3, 1, 4)) for t in (send_table, recv_table)), motion.T)
     dist_next, loads = pl.pallas_call(
-        functools.partial(stream_kernel, nz, ny),
-        grid=(nx // 2,),
+        functools.partial(stream_kernel, nx, nz, ny),
         out_shape=[jax.ShapeDtypeStruct(dist.shape, F32), jax.ShapeDtypeStruct((2, 6), F32)],
         in_specs=[vmem, vmem, vmem],
-        out_specs=[
-            pl.BlockSpec((19, 2, nz, ny), lambda step: (0, step, 0, 0)),
-            pl.BlockSpec((2, 6), lambda step: (0, 0)),
-        ],
-        compiler_params=pltpu.CompilerParams(vmem_limit_bytes=8 << 20),
+        out_specs=[hbm, vmem],
+        scratch_shapes=[pltpu.VMEM((19, nx, nz, ny), F32), dma((nx,))],
+        compiler_params=pltpu.CompilerParams(vmem_limit_bytes=12 << 20),
         name="stream",
     )(post, yin, total)
     return (dist_next, loads.T)

time: 42.6 us -> 33 us (0.77)
  Pallas kernels: 41.8 us -> 31.9 us
    pallas_call x1, Pallas kernels: 36.2 us -> 26.5 us  [per_device(): pl.pallas_call(functools.partial(step_kernel, (slabs, cols, nx, nz, ny, k...]
where the time goes in v1:
time: 33 us; the launch traced here: 32.5 us
  Pallas kernels  31.9 us (97%)
  between operations  0.64 us (2%)
    pallas_call x1, Pallas kernels, per_device(): pl.pallas_call(functools.partial(step_kernel, (slabs, cols, nx, nz, ny, k...  26.5 us
    pallas_call x1, Pallas kernels, per_device(): pl.pallas_call(functools.partial(stream_kernel, nx, nz, ny), out_shape=[j...  5.37 us

profile of v1, /device:TPU:1, one launch (start us, length us, event | category | flops | bytes accessed | tf_op | source)
XLA Modules:
  0.0 32.5 jit_solution(4825699406378729633)
XLA Ops:
  0.6 26.5 %collide_exchange.1 = (f32[19,18,64,128]{3,2,1,0:T(8,128)S(1)}, f32[2,64,128]{2,1,0:T(8,128)S(1)}, f32[16,128]{1,0:T(8,128)S(1)}) custom-call(f32[19,16,64,128]{3,2,1,0:T(8,128)} %dist_hbm.1, bf16[1,1,3,3,8,2,8,128]{7,6,5,4,3,2,1,0:T(8,128)(2,1)} %frac_hbm.1, s32[1,3,3,1,8]{4,3,2,1,0:T(1,128)} %bitcast.4, s32[1,3,3,1,8]{4,3,2,1,0:T(1,128)} %bitcast.5, ...), custom_call_target="tpu_custom_call" | custom-call | tf_op jit(solution)/shard_map/collide_exchange/pallas_call | solution.py:478
  27.2 5.4 %stream.1 = (f32[19,16,64,128]{3,2,1,0:T(8,128)}, f32[2,6]{1,0:T(2,128)}) custom-call(f32[19,18,64,128]{3,2,1,0:T(8,128)S(1)} %get-tuple-element.7.post_ref, f32[2,64,128]{2,1,0:T(8,128)S(1)} %get-tuple-element.8.yin_ref, f32[16,128]{1,0:T(8,128)S(1)} %get-tuple-element.9.total_ref), custom_call_target="tpu_custom_call" | custom-call | tf_op jit(solution)/shard_map/stream/pallas_call | solution.py:510

commit v2 on v1

--- a/solution.py
+++ b/solution.py
@@ -28,14 +28,15 @@
 FALLING = [4, 8, 9, 16, 18]
 CORNERS = [(7, 1, 1), (10, -1, 1), (9, 1, -1), (8, -1, -1)]
 OFFSETS = [(a, b) for a in range(3) for b in range(3) if (a, b) != (1, 1)]
+SEND_ORDER = [(0, 1), (2, 1), (0, 0), (2, 0), (0, 2), (2, 2), (1, 0), (1, 2)]
 N_FIELD = 7
 
 
 def step_kernel(
-    sizes, dist_hbm, frac_hbm, send_ref, recv_ref, motion_ref,
+    sizes, dist_hbm, frac_hbm, send_hbm, recv_hbm, motion_hbm,
     post_ref, yin_ref, total_ref,
     cells_buf, fluid_buf, frac_in, par_out, par_in, slot_buf, table_v, table_s,
-    ypack, corner_out, corner_in, part_out, part_in,
+    ypack, corner_out, corner_in, part_out, part_in, send_ref, recv_ref, motion_ref,
     dist_sem, frac_send, frac_recv, par_send, par_recv, local_sem,
     xr_send, xr_recv, yr_send, yr_recv, cr_send, cr_recv, ld_send, ld_recv,
 ):
@@ -54,7 +55,7 @@
         )
 
     def row_of(step):
-        return lax.rem(nbx - step, nbx)
+        return lax.rem(step + (nbx - 1), nbx)
 
     def dist_copy(step):
         rows = pl.ds(row_of(step) * 2, 2)
@@ -66,6 +67,14 @@
     for a, b in OFFSETS:
         pl.semaphore_signal(barrier, inc=1, device_id=at(a - 1, b - 1), device_id_type=MESH)
 
+    small = [
+        pltpu.make_async_copy(src, dst, local_sem.at[2 + n])
+        for n, (src, dst) in enumerate(
+            ((motion_hbm, motion_ref), (send_hbm, send_ref), (recv_hbm, recv_ref))
+        )
+    ]
+    for copy in small:
+        copy.start()
     for step in range(nbx):
         dist_copy(step).start()
     own_copy = pltpu.make_async_copy(frac_hbm.at[0, 0, 1, 1], frac_in.at[4], local_sem.at[0])
@@ -74,6 +83,8 @@
     lane = lax.broadcasted_iota(jnp.int32, (8, 128), 1)
     sub = lax.broadcasted_iota(jnp.int32, (8, 128), 0)
 
+    for copy in small:
+        copy.wait()
     base = jnp.zeros((8, 128), F32)
     for s in range(2):
         for r in range(9):
@@ -91,16 +102,17 @@
 
     pl.semaphore_wait(barrier, len(OFFSETS))
     payload = {}
-    for a, b in OFFSETS:
+    for a, b in SEND_ORDER:
         out, land = a * 3 + b, (2 - a) * 3 + (2 - b)
         payload[land] = (
+            remote(par_out.at[out], par_in.at[land],
+                   par_send.at[out], par_recv.at[land], a - 1, b - 1),
             remote(frac_hbm.at[0, 0, a, b], frac_in.at[land],
                    frac_send.at[out], frac_recv.at[land], a - 1, b - 1),
-            remote(par_out.at[out], par_in.at[land],
-                   par_send.at[out], par_recv.at[land], a - 1, b - 1),
         )
-        for copy in payload[land]:
-            copy.start()
+    for part in range(2):
+        for pair in payload.values():
+            pair[part].start()
 
     first = jnp.full((8, 128), slots, jnp.int32)
     other = jnp.full((8, 128), slots, jnp.int32)
@@ -180,20 +192,7 @@
     def rounded(value):
         return value.astype(jnp.bfloat16).astype(F32)
 
-    def slots_of(step, _):
-        n = lax.rem(step + 3, 9)
-
-        @pl.when(step == 0)
-        def _():
-            own_copy.wait()
-
-        for group in range(3):
-            @pl.when(step == 3 * group)
-            def _():
-                for land in range(3 * ((group + 1) % 3), 3 * ((group + 1) % 3) + 3):
-                    for copy in payload.get(land, ()):
-                        copy.wait_recv()
-
+    def slots_of(n):
         row = par_in[n]
         both = [spread(row, r) for r in range(18)]
         for j in range(kd):
@@ -209,9 +208,21 @@
                 slot_buf[slot, dx] = jnp.where(live, weight, 0.0)
                 slot_buf[slot, 3 + dx] = rounded(vy + (wz * lever_x[dx] - wx * lever_z))
                 slot_buf[slot, 5 + dx] = rounded(vz + (wx * lever_y - wy * lever_x[dx]))
+
+    def slots_group(group, _):
+        start = lax.rem(3 + 6 * group, 9)
+        for g, lands in enumerate(((3, 5), (0, 1, 2), (6, 7, 8))):
+            @pl.when(group == g)
+            def _():
+                for land in lands:
+                    for copy in payload[land]:
+                        copy.wait_recv()
+        for n in range(3):
+            slots_of(start + n)
         return 0
 
-    lax.fori_loop(0, 9, slots_of, 0)
+    own_copy.wait()
+    lax.fori_loop(0, 3, slots_group, 0)
     table_copy.wait()
 
     def collide_block(bx, bz):
@@ -276,40 +287,18 @@
 
     lane_z = lax.broadcasted_iota(jnp.int32, (nz, 128), 1)
 
-    def pack_row(bx):
-        start = (2 * bx + 1) * 5
-        mine = (lane_z >= start) & (lane_z < start + 10)
+    def pack_pair(pair):
         for way, (pops, edge) in enumerate(((RISING, 127), (FALLING, 0))):
-            packed = jnp.zeros((nz, 128), F32)
-            for dx in range(2):
-                for m in range(5):
-                    plane = post_ref[SLOT[pops[m]], bx * 2 + dx + 1]
-                    place = dx * 5 + m
-                    shift = (place - edge) % 128
-                    packed = jnp.where(
-                        lane_z == place, plane if shift == 0 else pltpu.roll(plane, shift, 1), packed
-                    )
-            ypack[way] = jnp.where(mine, pltpu.roll(packed, start, 1), ypack[way])
-
-    def collide_row(step, _):
-        bx = row_of(step)
-
-        def body(bz, _):
-            collide_block(bx, bz)
-            return 0
-
-        lax.fori_loop(0, nbz, body, 0)
-
-        @pl.when(step == 0)
-        def _():
-            x_copies[1].start()
-
-        @pl.when(step == 1)
-        def _():
-            x_copies[0].start()
-
-        pack_row(bx)
-        return 0
+            packed = ypack[way]
+            for half in range(2):
+                bx = row_of(2 * pair + half)
+                for dx in range(2):
+                    for m in range(5):
+                        plane = post_ref[SLOT[pops[m]], bx * 2 + dx + 1]
+                        place = (2 * bx + dx + 1) * 5 + m
+                        turned = pltpu.roll(plane, lax.rem(place + (128 - edge), 128), 1)
+                        packed = jnp.where(lane_z == place, turned, packed)
+            ypack[way] = packed
 
     x_copies = [
         remote(post_ref.at[pl.ds(0, 5), nx], post_ref.at[pl.ds(0, 5), 0],
@@ -317,7 +306,20 @@
         remote(post_ref.at[pl.ds(5, 5), 1], post_ref.at[pl.ds(5, 5), nx + 1],
                xr_send.at[1], xr_recv.at[1], -1, 0),
     ]
-    lax.fori_loop(0, 2, collide_row, 0)
+
+    def collide_pair(pair, _):
+        def body(i, _):
+            collide_block(row_of(2 * pair + i // nbz), lax.rem(i, nbz))
+
+            for n in range(2):
+                @pl.when((pair == 0) & (i == nbz * (n + 1) - 1))
+                def _():
+                    x_copies[n].start()
+            return 0
+
+        return lax.fori_loop(0, 2 * nbz, body, 0)
+
+    collide_pair(0, 0)
 
     corner_copies = []
     for n, (pop, sx, sy) in enumerate(CORNERS):
@@ -332,7 +334,7 @@
         copy.start()
         corner_copies.append(copy)
 
-    def loads_of(n, _):
+    def loads_of(n):
         row = par_in[n]
         both = [spread(row, 9 * s + r) for s in range(2) for r in range(3)]
         acc = [jnp.zeros((8, 128), F32) for _ in range(12)]
@@ -367,18 +369,30 @@
                 total = jnp.sum(acc[6 * s + c], axis=0, keepdims=True)
                 stack = jnp.where(sub == c, total, stack)
             part_out[n, pl.ds(8 * s, 8), :] = stack
+
+    def loads_group(group, _):
+        for n in range(3):
+            loads_of(3 * group + n)
         return 0
 
-    lax.fori_loop(0, 9, loads_of, 0)
+    pack_pair(0)
+
+    def other_pair(pair, _):
+        collide_pair(pair, 0)
+        pack_pair(pair)
+        return 0
+
+    other_pair(1, 0)
+    lax.fori_loop(0, 3, loads_group, 0)
     load_copies = []
-    for a, b in OFFSETS:
+    for a, b in SEND_ORDER:
         out, land = a * 3 + b, (2 - a) * 3 + (2 - b)
         copy = remote(part_out.at[out], part_in.at[land],
                       ld_send.at[out], ld_recv.at[land], a - 1, b - 1)
         copy.start()
         load_copies.append((land, copy))
 
-    lax.fori_loop(2, nbx, collide_row, 0)
+    lax.fori_loop(2, nbx // 2, other_pair, 0)
 
     y_copies = [
         remote(ypack.at[0], yin_ref.at[0], yr_send.at[0], yr_recv.at[0], 0, 1),
@@ -387,13 +401,7 @@
     for copy in y_copies:
         copy.start()
 
-    total = part_out[4]
-    for land, copy in load_copies:
-        copy.wait_recv()
-        total = total + part_in[land]
-    total_ref[...] = total
-
-    for copy in corner_copies + y_copies + x_copies:
+    for copy in corner_copies + y_copies:
         copy.wait_recv()
     for n, (pop, sx, sy) in enumerate(CORNERS):
         way = 0 if sy == 1 else 1
@@ -404,6 +412,14 @@
             moved = pltpu.roll(line, (place - bz) % 128, 1)
             yin_ref[way, rows, :] = jnp.where(lane == place, moved, yin_ref[way, rows, :])
 
+    total = part_out[4]
+    for land, copy in load_copies:
+        copy.wait_recv()
+        total = total + part_in[land]
+    total_ref[...] = total
+    for copy in x_copies:
+        copy.wait_recv()
+
     for pair in payload.values():
         for copy in pair:
             copy.wait_send()
@@ -414,7 +430,7 @@
 
 
 def stream_kernel(
-    nx, nz, ny, post_ref, yin_ref, total_ref, out_hbm, loads_ref, planes, out_sem
+    nx, nz, ny, post_ref, yin_ref, total_ref, out_hbm, loads_hbm, planes, loads_ref, out_sem
 ):
     lane = lax.broadcasted_iota(jnp.int32, (nz, ny), 1)
     row = lax.broadcasted_iota(jnp.int32, (nz, ny), 0)
@@ -447,7 +463,7 @@
         copy_out(x).start()
         return 0
 
-    lax.fori_loop(0, nx, plane_of, 0)
+    lax.fori_loop(0, nx, plane_of, 0, unroll=4)
     total = jnp.sum(total_ref[...], axis=1, keepdims=True) * (-1.0 / (2 * 8 * ny))
     place_s = lax.broadcasted_iota(jnp.int32, (2, 6), 0)
     place_c = lax.broadcasted_iota(jnp.int32, (2, 6), 1)
@@ -457,12 +473,15 @@
             value = jnp.broadcast_to(total[8 * s + c:8 * s + c + 1], (2, 6))
             result = jnp.where((place_s == s) & (place_c == c), value, result)
     loads_ref[...] = result
+    loads_copy = pltpu.make_async_copy(loads_ref, loads_hbm, out_sem.at[nx])
+    loads_copy.start()
 
     def finish(x, _):
         copy_out(x).wait()
         return 0
 
     lax.fori_loop(0, nx, finish, 0)
+    loads_copy.wait()
 
 
 def per_device(mesh_sizes, dist, fraction, send_table, recv_table, motion):
@@ -472,7 +491,6 @@
     slots = 9 * kd
     blocks = (nx // 2) * (nz // 8)
     hbm = pl.BlockSpec(memory_space=pltpu.HBM)
-    smem = pl.BlockSpec(memory_space=pltpu.SMEM)
     vmem = pl.BlockSpec(memory_space=pltpu.VMEM)
     dma = pltpu.SemaphoreType.DMA
     post, yin, total = pl.pallas_call(
@@ -482,7 +500,7 @@
             pltpu.VMEM((2, nz, ny), F32),
             pltpu.VMEM((16, 128), F32),
         ],
-        in_specs=[hbm, hbm, smem, smem, smem],
+        in_specs=[hbm] * 5,
         out_specs=[vmem, vmem, vmem],
         scratch_shapes=[
             pltpu.VMEM((19, nx, nz, ny), F32),
@@ -498,7 +516,10 @@
             pltpu.VMEM((4, 8, 128), F32),
             pltpu.VMEM((9, 16, 128), F32),
             pltpu.VMEM((9, 16, 128), F32),
-            dma((nx // 2,)), dma((9,)), dma((9,)), dma((9,)), dma((9,)), dma((2,)),
+            pltpu.SMEM((1, 3, 3, 1, kd), jnp.int32),
+            pltpu.SMEM((1, 3, 3, 1, kd), jnp.int32),
+            pltpu.SMEM((2, 9), F32),
+            dma((nx // 2,)), dma((9,)), dma((9,)), dma((9,)), dma((9,)), dma((5,)),
             dma((2,)), dma((2,)), dma((2,)), dma((2,)), dma((4,)), dma((4,)),
             dma((9,)), dma((9,)),
         ],
@@ -511,8 +532,10 @@
         functools.partial(stream_kernel, nx, nz, ny),
         out_shape=[jax.ShapeDtypeStruct(dist.shape, F32), jax.ShapeDtypeStruct((2, 6), F32)],
         in_specs=[vmem, vmem, vmem],
-        out_specs=[hbm, vmem],
-        scratch_shapes=[pltpu.VMEM((19, nx, nz, ny), F32), dma((nx,))],
+        out_specs=[hbm, hbm],
+        scratch_shapes=[
+            pltpu.VMEM((19, nx, nz, ny), F32), pltpu.VMEM((2, 6), F32), dma((nx + 1,))
+        ],
         compiler_params=pltpu.CompilerParams(vmem_limit_bytes=12 << 20),
         name="stream",
     )(post, yin, total)

time: 33 us -> 30.6 us (0.927)
  Pallas kernels: 31.9 us -> 29.8 us
    pallas_call x1, Pallas kernels: 5.37 us -> 4.15 us  [per_device(): pl.pallas_call(functools.partial(stream_kernel, nx, nz, ny), out_shape=[j...]
    pallas_call x1, Pallas kernels: 26.5 us -> 25.7 us  [per_device(): pl.pallas_call(functools.partial(step_kernel, (slabs, cols, nx, nz, ny, k...]
where the time goes in v2:
time: 30.6 us; the launch traced here: 30.4 us
  Pallas kernels  29.8 us (97%)
  between operations  0.64 us (2%)
    pallas_call x1, Pallas kernels, per_device(): pl.pallas_call(functools.partial(step_kernel, (slabs, cols, nx, nz, ny, k...  25.7 us
    pallas_call x1, Pallas kernels, per_device(): pl.pallas_call(functools.partial(stream_kernel, nx, nz, ny), out_shape=[j...  4.15 us

profile of v2, /device:TPU:1, one launch (start us, length us, event | category | flops | bytes accessed | tf_op | source)
XLA Modules:
  0.0 30.4 jit_solution(3422598794427042237)
XLA Ops:
  0.6 25.7 %collide_exchange.1 = (f32[19,18,64,128]{3,2,1,0:T(8,128)S(1)}, f32[2,64,128]{2,1,0:T(8,128)S(1)}, f32[16,128]{1,0:T(8,128)S(1)}) custom-call(f32[19,16,64,128]{3,2,1,0:T(8,128)} %dist_hbm.1, bf16[1,1,3,3,8,2,8,128]{7,6,5,4,3,2,1,0:T(8,128)(2,1)} %frac_hbm.1, s32[1,3,3,1,8]{4,3,2,1,0:T(1,128)} %bitcast.4, s32[1,3,3,1,8]{4,3,2,1,0:T(1,128)} %bitcast.5, ...), custom_call_target="tpu_custom_call" | custom-call | tf_op jit(solution)/shard_map/collide_exchange/pallas_call | solution.py:496
  26.3 4.2 %stream.1 = (f32[19,16,64,128]{3,2,1,0:T(8,128)}, f32[2,6]{1,0:T(2,128)}) custom-call(f32[19,18,64,128]{3,2,1,0:T(8,128)S(1)} %get-tuple-element.7.post_ref, f32[2,64,128]{2,1,0:T(8,128)S(1)} %get-tuple-element.8.yin_ref, f32[16,128]{1,0:T(8,128)S(1)} %get-tuple-element.9.total_ref), custom_call_target="tpu_custom_call" | custom-call | tf_op jit(solution)/shard_map/stream/pallas_call | solution.py:531

commit v3 on v2

--- a/solution.py
+++ b/solution.py
@@ -307,19 +307,35 @@
                xr_send.at[1], xr_recv.at[1], -1, 0),
     ]
 
-    def collide_pair(pair, _):
-        def body(i, _):
+    def pack_tile(pair, bz):
+        rows = pl.ds(pl.multiple_of(bz * 8, 8), 8)
+        for way, (pops, edge) in enumerate(((RISING, 127), (FALLING, 0))):
+            packed = ypack[way, rows, :]
+            for half in range(2):
+                bx = row_of(2 * pair + half)
+                for dx in range(2):
+                    for m in range(5):
+                        part = post_ref[SLOT[pops[m]], bx * 2 + dx + 1, rows, :]
+                        place = (2 * bx + dx + 1) * 5 + m
+                        turned = pltpu.roll(part, lax.rem(place + (128 - edge), 128), 1)
+                        packed = jnp.where(lane == place, turned, packed)
+            ypack[way, rows, :] = packed
+
+    def collide_two(pair, t):
+        for u in range(2):
+            i = 2 * t + u
             collide_block(row_of(2 * pair + i // nbz), lax.rem(i, nbz))
 
-            for n in range(2):
-                @pl.when((pair == 0) & (i == nbz * (n + 1) - 1))
-                def _():
-                    x_copies[n].start()
-            return 0
-
-        return lax.fori_loop(0, 2 * nbz, body, 0)
-
-    collide_pair(0, 0)
+    def first_pair(t, _):
+        collide_two(0, t)
+
+        for n in range(2):
+            @pl.when(2 * t + 2 == nbz * (n + 1))
+            def _():
+                x_copies[n].start()
+        return 0
+
+    lax.fori_loop(0, nbz, first_pair, 0)
 
     corner_copies = []
     for n, (pop, sx, sy) in enumerate(CORNERS):
@@ -375,12 +391,13 @@
             loads_of(3 * group + n)
         return 0
 
-    pack_pair(0)
-
     def other_pair(pair, _):
-        collide_pair(pair, 0)
-        pack_pair(pair)
-        return 0
+        def body(t, _):
+            pack_tile(pair - 1, t)
+            collide_two(pair, t)
+            return 0
+
+        return lax.fori_loop(0, nbz, body, 0)
 
     other_pair(1, 0)
     lax.fori_loop(0, 3, loads_group, 0)
@@ -393,6 +410,7 @@
         load_copies.append((land, copy))
 
     lax.fori_loop(2, nbx // 2, other_pair, 0)
+    pack_pair(nbx // 2 - 1)
 
     y_copies = [
         remote(ypack.at[0], yin_ref.at[0], yr_send.at[0], yr_recv.at[0], 0, 1),

time: 30.6 us -> 29.7 us (0.971)
  Pallas kernels: 29.8 us -> 28.7 us
    pallas_call x1, Pallas kernels: 25.7 us -> 24.6 us  [per_device(): pl.pallas_call(functools.partial(step_kernel, (slabs, cols, nx, nz, ny, k...]
where the time goes in v3:
time: 29.7 us; the launch traced here: 29.3 us
  Pallas kernels  28.7 us (97%)
  between operations  0.64 us (2%)
    pallas_call x1, Pallas kernels, per_device(): pl.pallas_call(functools.partial(step_kernel, (slabs, cols, nx, nz, ny, k...  24.6 us
    pallas_call x1, Pallas kernels, per_device(): pl.pallas_call(functools.partial(stream_kernel, nx, nz, ny), out_shape=[j...  4.15 us

profile of v3, /device:TPU:1, one launch (start us, length us, event | category | flops | bytes accessed | tf_op | source)
XLA Modules:
  0.0 29.3 jit_solution(12040449742054778546)
XLA Ops:
  0.6 24.6 %collide_exchange.1 = (f32[19,18,64,128]{3,2,1,0:T(8,128)S(1)}, f32[2,64,128]{2,1,0:T(8,128)S(1)}, f32[16,128]{1,0:T(8,128)S(1)}) custom-call(f32[19,16,64,128]{3,2,1,0:T(8,128)} %dist_hbm.1, bf16[1,1,3,3,8,2,8,128]{7,6,5,4,3,2,1,0:T(8,128)(2,1)} %frac_hbm.1, s32[1,3,3,1,8]{4,3,2,1,0:T(1,128)} %bitcast.4, s32[1,3,3,1,8]{4,3,2,1,0:T(1,128)} %bitcast.5, ...), custom_call_target="tpu_custom_call" | custom-call | tf_op jit(solution)/shard_map/collide_exchange/pallas_call | solution.py:514
  25.2 4.2 %stream.1 = (f32[19,16,64,128]{3,2,1,0:T(8,128)}, f32[2,6]{1,0:T(2,128)}) custom-call(f32[19,18,64,128]{3,2,1,0:T(8,128)S(1)} %get-tuple-element.7.post_ref, f32[2,64,128]{2,1,0:T(8,128)S(1)} %get-tuple-element.8.yin_ref, f32[16,128]{1,0:T(8,128)S(1)} %get-tuple-element.9.total_ref), custom_call_target="tpu_custom_call" | custom-call | tf_op jit(solution)/shard_map/stream/pallas_call | solution.py:549

commit v4 on v3

--- a/solution.py
+++ b/solution.py
@@ -30,6 +30,7 @@
 OFFSETS = [(a, b) for a in range(3) for b in range(3) if (a, b) != (1, 1)]
 SEND_ORDER = [(0, 1), (2, 1), (0, 0), (2, 0), (0, 2), (2, 2), (1, 0), (1, 2)]
 N_FIELD = 7
+PRODUCTS = [(0, 0), (1, 1), (2, 2), (0, 1), (0, 2), (1, 2)]
 
 
 def step_kernel(
@@ -154,10 +155,14 @@
                 mom_y = (minus[3] + (minus[7] - minus[9])) + (minus[15] + minus[17])
                 mom_z = (minus[5] + (minus[11] - minus[13])) + (minus[15] - minus[17])
                 block = bx * nbz + bz
+                mom = [mom_x, mom_y, mom_z]
+                vel = [m * inverse for m in mom]
                 fluid_buf[block, 0, dx] = density
-                fluid_buf[block, 1, dx] = mom_x * inverse
-                fluid_buf[block, 2, dx] = mom_y * inverse
-                fluid_buf[block, 3, dx] = mom_z * inverse
+                for c in range(3):
+                    fluid_buf[block, 1 + c, dx] = vel[c]
+                    fluid_buf[block, 4 + c, dx] = mom[c]
+                for n, (c, d) in enumerate(PRODUCTS):
+                    fluid_buf[block, 7 + n, dx] = mom[c] * vel[d]
             return 0
 
         return lax.fori_loop(0, nbz, moments_block, 0)
@@ -231,33 +236,25 @@
         one, two = table_s[0, 0, block], table_s[1, 0, block]
         for dx in range(2):
             x = bx * 2 + dx
+            density = fluid_buf[block, 0, dx]
+            weights = [slot_buf[slot, dx] for slot in (one, two)]
+            solid = weights[0] + weights[1]
             fields = []
-            for slot in (one, two):
-                weight = slot_buf[slot, dx]
+            for slot, weight in zip((one, two), weights):
                 flow = [slot_buf[slot, 2], slot_buf[slot, 3 + dx], slot_buf[slot, 5 + dx]]
-                first_m = [weight * f for f in flow]
-                second_m = [
-                    first_m[0] * flow[0], first_m[1] * flow[1], first_m[2] * flow[2],
-                    first_m[0] * flow[1], first_m[0] * flow[2], first_m[1] * flow[2],
-                ]
-                fields.append([weight] + first_m + second_m)
+                mass = weight * density
+                first_m = [mass * f for f in flow]
+                fields.append(first_m + [first_m[c] * flow[d] for c, d in PRODUCTS])
             total = [u + v for u, v in zip(*fields)]
-            solid = total[0]
-            density = fluid_buf[block, 0, dx]
-            vel = [fluid_buf[block, 1 + c, dx] for c in range(3)]
             relax = (1.0 - solid) * (1.0 / TAU)
             keep = 0.5 - 0.5 * relax
             keep_odd = keep - solid
-            even_rho = (relax - solid) * density
-            odd_rho = (relax + solid) * density
-            scaled = [even_rho * v for v in vel]
-            flux = [odd_rho * vel[c] + density * total[1 + c] for c in range(3)]
-            t_xx = scaled[0] * vel[0] + density * total[4]
-            t_yy = scaled[1] * vel[1] + density * total[5]
-            t_zz = scaled[2] * vel[2] + density * total[6]
-            t_xy = scaled[0] * vel[1] + density * total[7]
-            t_xz = scaled[0] * vel[2] + density * total[8]
-            t_yz = scaled[1] * vel[2] + density * total[9]
+            even_part = relax - solid
+            odd_part = relax + solid
+            flux = [odd_part * fluid_buf[block, 4 + c, dx] + total[c] for c in range(3)]
+            t_xx, t_yy, t_zz, t_xy, t_xz, t_yz = [
+                even_part * fluid_buf[block, 7 + n, dx] + total[3 + n] for n in range(6)
+            ]
             rest = relax * density - 1.5 * ((t_xx + t_yy) + t_zz)
             outs = {0: (keep + keep) * cells_buf[0, x, rows, :] + (1.0 / 3.0) * rest}
             rest_axis = (1.0 / 18.0) * rest
@@ -393,11 +390,13 @@
 
     def other_pair(pair, _):
         def body(t, _):
-            pack_tile(pair - 1, t)
-            collide_two(pair, t)
+            for u in range(2):
+                pack_tile(pair - 1, 2 * t + u)
+            for u in range(2):
+                collide_two(pair, 2 * t + u)
             return 0
 
-        return lax.fori_loop(0, nbz, body, 0)
+        return lax.fori_loop(0, nbz // 2, body, 0)
 
     other_pair(1, 0)
     lax.fori_loop(0, 3, loads_group, 0)
@@ -408,7 +407,6 @@
                       ld_send.at[out], ld_recv.at[land], a - 1, b - 1)
         copy.start()
         load_copies.append((land, copy))
-
     lax.fori_loop(2, nbx // 2, other_pair, 0)
     pack_pair(nbx // 2 - 1)
 
@@ -522,7 +520,7 @@
         out_specs=[vmem, vmem, vmem],
         scratch_shapes=[
             pltpu.VMEM((19, nx, nz, ny), F32),
-            pltpu.VMEM((blocks, 4, 2, 8, ny), F32),
+            pltpu.VMEM((blocks, 13, 2, 8, ny), F32),
             pltpu.VMEM((9, kd, 2, 8, ny), jnp.bfloat16),
             pltpu.VMEM((9, 8, 128), F32),
             pltpu.VMEM((9, 8, 128), F32),

time: 29.7 us -> 29.2 us (0.983)
  no operation moved by 1% of the time
where the time goes in v4:
time: 29.2 us; the launch traced here: 29.1 us
  Pallas kernels  28.5 us (98%)
  between operations  0.64 us (2%)
    pallas_call x1, Pallas kernels, per_device(): pl.pallas_call(functools.partial(step_kernel, (slabs, cols, nx, nz, ny, k...  24.3 us
    pallas_call x1, Pallas kernels, per_device(): pl.pallas_call(functools.partial(stream_kernel, nx, nz, ny), out_shape=[j...  4.15 us

profile of v4, /device:TPU:1, one launch (start us, length us, event | category | flops | bytes accessed | tf_op | source)
XLA Modules:
  0.0 29.1 jit_solution(18304604950247692903)
XLA Ops:
  0.6 24.3 %collide_exchange.1 = (f32[19,18,64,128]{3,2,1,0:T(8,128)S(1)}, f32[2,64,128]{2,1,0:T(8,128)S(1)}, f32[16,128]{1,0:T(8,128)S(1)}) custom-call(f32[19,16,64,128]{3,2,1,0:T(8,128)} %dist_hbm.1, bf16[1,1,3,3,8,2,8,128]{7,6,5,4,3,2,1,0:T(8,128)(2,1)} %frac_hbm.1, s32[1,3,3,1,8]{4,3,2,1,0:T(1,128)} %bitcast.4, s32[1,3,3,1,8]{4,3,2,1,0:T(1,128)} %bitcast.5, ...), custom_call_target="tpu_custom_call" | custom-call | tf_op jit(solution)/shard_map/collide_exchange/pallas_call | solution.py:512
  24.9 4.2 %stream.1 = (f32[19,16,64,128]{3,2,1,0:T(8,128)}, f32[2,6]{1,0:T(2,128)}) custom-call(f32[19,18,64,128]{3,2,1,0:T(8,128)S(1)} %get-tuple-element.7.post_ref, f32[2,64,128]{2,1,0:T(8,128)S(1)} %get-tuple-element.8.yin_ref, f32[16,128]{1,0:T(8,128)S(1)} %get-tuple-element.9.total_ref), custom_call_target="tpu_custom_call" | custom-call | tf_op jit(solution)/shard_map/stream/pallas_call | solution.py:547

commit v5 on v4

--- a/solution.py
+++ b/solution.py
@@ -284,8 +284,9 @@
 
     lane_z = lax.broadcasted_iota(jnp.int32, (nz, 128), 1)
 
-    def pack_pair(pair):
-        for way, (pops, edge) in enumerate(((RISING, 127), (FALLING, 0))):
+    def pack_pair(pair, ways):
+        for way in ways:
+            pops, edge = ((RISING, 127), (FALLING, 0))[way]
             packed = ypack[way]
             for half in range(2):
                 bx = row_of(2 * pair + half)
@@ -383,9 +384,22 @@
                 stack = jnp.where(sub == c, total, stack)
             part_out[n, pl.ds(8 * s, 8), :] = stack
 
+    load_copies = {}
+    for a, b in SEND_ORDER:
+        out, land = a * 3 + b, (2 - a) * 3 + (2 - b)
+        load_copies[out] = (land, remote(
+            part_out.at[out], part_in.at[land], ld_send.at[out], ld_recv.at[land], a - 1, b - 1
+        ))
+
     def loads_group(group, _):
+        start = lax.rem(6 * group, 9)
         for n in range(3):
-            loads_of(3 * group + n)
+            loads_of(start + n)
+        for g, outs in enumerate(((0, 1, 2), (6, 7, 8), (3, 5))):
+            @pl.when(group == g)
+            def _():
+                for out in outs:
+                    load_copies[out][1].start()
         return 0
 
     def other_pair(pair, _):
@@ -400,22 +414,15 @@
 
     other_pair(1, 0)
     lax.fori_loop(0, 3, loads_group, 0)
-    load_copies = []
-    for a, b in SEND_ORDER:
-        out, land = a * 3 + b, (2 - a) * 3 + (2 - b)
-        copy = remote(part_out.at[out], part_in.at[land],
-                      ld_send.at[out], ld_recv.at[land], a - 1, b - 1)
-        copy.start()
-        load_copies.append((land, copy))
     lax.fori_loop(2, nbx // 2, other_pair, 0)
-    pack_pair(nbx // 2 - 1)
 
     y_copies = [
         remote(ypack.at[0], yin_ref.at[0], yr_send.at[0], yr_recv.at[0], 0, 1),
         remote(ypack.at[1], yin_ref.at[1], yr_send.at[1], yr_recv.at[1], 0, -1),
     ]
-    for copy in y_copies:
-        copy.start()
+    for way in range(2):
+        pack_pair(nbx // 2 - 1, (way,))
+        y_copies[way].start()
 
     for copy in corner_copies + y_copies:
         copy.wait_recv()
@@ -429,7 +436,7 @@
             yin_ref[way, rows, :] = jnp.where(lane == place, moved, yin_ref[way, rows, :])
 
     total = part_out[4]
-    for land, copy in load_copies:
+    for land, copy in load_copies.values():
         copy.wait_recv()
         total = total + part_in[land]
     total_ref[...] = total
@@ -441,7 +448,7 @@
             copy.wait_send()
     for copy in x_copies + corner_copies + y_copies:
         copy.wait_send()
-    for _, copy in load_copies:
+    for _, copy in load_copies.values():
         copy.wait_send()
 
 

time: 29.2 us -> 29 us (level)
  Pallas kernels: 28.5 us -> 28.2 us
where the time goes in v5:
time: 29 us; the launch traced here: 28.9 us
  Pallas kernels  28.2 us (97%)
  between operations  0.64 us (2%)
    pallas_call x1, Pallas kernels, per_device(): pl.pallas_call(functools.partial(step_kernel, (slabs, cols, nx, nz, ny, k...  24.1 us
    pallas_call x1, Pallas kernels, per_device(): pl.pallas_call(functools.partial(stream_kernel, nx, nz, ny), out_shape=[j...  4.15 us

profile of v5, /device:TPU:1, one launch (start us, length us, event | category | flops | bytes accessed | tf_op | source)
XLA Modules:
  0.0 28.9 jit_solution(8049277002761286437)
XLA Ops:
  0.6 24.1 %collide_exchange.1 = (f32[19,18,64,128]{3,2,1,0:T(8,128)S(1)}, f32[2,64,128]{2,1,0:T(8,128)S(1)}, f32[16,128]{1,0:T(8,128)S(1)}) custom-call(f32[19,16,64,128]{3,2,1,0:T(8,128)} %dist_hbm.1, bf16[1,1,3,3,8,2,8,128]{7,6,5,4,3,2,1,0:T(8,128)(2,1)} %frac_hbm.1, s32[1,3,3,1,8]{4,3,2,1,0:T(1,128)} %bitcast.4, s32[1,3,3,1,8]{4,3,2,1,0:T(1,128)} %bitcast.5, ...), custom_call_target="tpu_custom_call" | custom-call | tf_op jit(solution)/shard_map/collide_exchange/pallas_call | solution.py:519
  24.7 4.2 %stream.1 = (f32[19,16,64,128]{3,2,1,0:T(8,128)}, f32[2,6]{1,0:T(2,128)}) custom-call(f32[19,18,64,128]{3,2,1,0:T(8,128)S(1)} %get-tuple-element.7.post_ref, f32[2,64,128]{2,1,0:T(8,128)S(1)} %get-tuple-element.8.yin_ref, f32[16,128]{1,0:T(8,128)S(1)} %get-tuple-element.9.total_ref), custom_call_target="tpu_custom_call" | custom-call | tf_op jit(solution)/shard_map/stream/pallas_call | solution.py:554
